TPU v7x, 32 devices: a whole 2x2x4 slice. The times are simulated.
32 devices in a mesh: segment: 4 (over y, x), chan: 8 (over z, core).
Axes of the slice: x: 2, y: 2, z: 4, core: 2. Of those that a mesh axis runs over, the one named last changes fastest.
Arguments:
- resident: float32 [4, 1280, 512], P('segment', 'chan'), may hold values from -6 to 6
- held_skip: float32 [4, 1280, 512], P('segment', 'chan'), may hold values from -6 to 6
- fresh: float32 [2, 1280, 512], P(None, 'chan'), may hold values from -6 to 6
- first_weight: float32 [4, 1280, 11520], P('segment', 'chan'), may hold values from -0.0546875 to 0.0546875
- second_weight: float32 [4, 1280, 11520], P('segment', 'chan'), may hold values from -0.0546875 to 0.0546875
Outputs:
- last_outputs: float32 [4, 1280, 512], P('segment', 'chan')
All inputs are finite; a program needn't handle non-finite values.
Results may differ from a plain program's by a relative error of at most 0.0001.
Values sent between devices are 32-bit elements; how exact they have to be, the bound alone decides.
A program may use at most 128 MiB of HBM per device.

v0:
```python
import jax
import jax.numpy as jnp
from jax import lax
from jax.sharding import PartitionSpec as P

ROWS = 16
COLS = 32
TICKS = 3


def passed_along(array, axis, by):
    length = lax.axis_size(axis)
    pairs = [(i, i + by) for i in range(length) if 0 <= i + by < length]
    return lax.ppermute(array, axis, pairs)


def tap_shift(field, dy, dx):
    grid = field.reshape(field.shape[:-1] + (ROWS, COLS))
    padded = jnp.pad(grid, [(0, 0)] * (grid.ndim - 2) + [(1, 1), (1, 1)])
    moved = padded[..., 1 + dy : 1 + dy + ROWS, 1 + dx : 1 + dx + COLS]
    return moved.reshape(field.shape)


def place_taps(parts):
    total = jnp.zeros((parts.shape[0], parts.shape[2]), jnp.float32)
    for dy in (-1, 0, 1):
        for dx in (-1, 0, 1):
            total = total + tap_shift(parts[:, 3 * (dy + 1) + (dx + 1)], dy, dx)
    return total


def make_fold(weight):
    out_rows = weight.shape[0]
    width = weight.shape[1] // 9
    taps = weight.reshape(out_rows, 9, width)

    def add_piece(total, piece, start):
        columns = taps
        columns = columns.reshape(out_rows * 9, piece.shape[0])
        return jnp.dot(
            columns, piece, precision=lax.Precision.HIGHEST, preferred_element_type=jnp.float32
        )

    return add_piece


def body(resident, held_skip, fresh, first_weight, second_weight):
    segment_index = lax.axis_index("segment")
    segments = lax.axis_size("segment")
    encoder = segment_index < segments // 2
    first = first_weight[0]
    second = second_weight[0]
    field = resident[0]
    skip = held_skip[0]
    out_rows = first.shape[0]
    positions = field.shape[1]
    fold_first = make_fold(first)
    fold_second = make_fold(second)
    empty = jnp.zeros((out_rows * 9, positions), jnp.float32)
    output = field
    for tick in range(TICKS):
        raw_first = fold_first(
            empty, lax.all_gather(field, "chan", axis=0, tiled=True), jnp.int32(0)
        )
        conv_first = place_taps(raw_first.reshape(out_rows, 9, positions))
        operand = jnp.where(encoder, jax.nn.silu(conv_first), skip)
        raw_second = fold_second(
            empty, lax.all_gather(operand, "chan", axis=0, tiled=True), jnp.int32(0)
        )
        conv_second = place_taps(raw_second.reshape(out_rows, 9, positions))
        output = jnp.where(encoder, field + conv_second, jax.nn.silu(conv_first + conv_second))
        if tick < TICKS - 1:
            passed = passed_along(output, "segment", 1)
            field = jnp.where(segment_index == 0, fresh[tick], passed)
            every_output = lax.all_gather(output[None], "segment", axis=0, tiled=True)
            mirrored = lax.dynamic_index_in_dim(
                every_output, segments - 1 - segment_index, 0, keepdims=False
            )
            skip = jnp.where(encoder, skip, mirrored)
    return output[None]


def solution(mesh):
    return jax.shard_map(
        body,
        mesh=mesh,
        in_specs=(
            P("segment", "chan", None),
            P("segment", "chan", None),
            P(None, "chan", None),
            P("segment", "chan", None),
            P("segment", "chan", None),
        ),
        out_specs=P("segment", "chan", None),
        check_vma=False,
    )
```

profile of v0, /device:TPU:0, one launch (start us, length us, event | category | flops | bytes accessed | tf_op | source)
XLA Modules:
  0.0 491.1 jit_solution(17155286248517563700)
XLA Ops:
  7.3 9.2 %dot_general.30 = f32[160,9,1280]{2,1,0:T(8,128)} reshape(f32[1,160,11520]{2,1,0:T(8,128)} %param.8) | data formatting | bytes 14745600 | tf_op jit(solution)/shard_map/dot_general | solution.py:40
  16.5 28.9 %all-gather.23.cloned.1.call-done = f32[1,1280,512]{2,1,0:T(8,128)} async-done(((f32[1,160,512]{2,1,0:T(8,128)}), f32[1,1280,512]{2,1,0:T(8,128)}) %all-gather.23.cloned.1.call-update) | async-done | bytes 2621456 | tf_op jit(solution)/shard_map/all_gather | solution.py:63
  45.4 19.8 %fusion = f32[160,9,512]{2,0,1:T(8,128)S(1)} fusion(f32[160,9,1280]{2,1,0:T(8,128)} %dot_general.30, f32[1,1280,512]{2,1,0:T(8,128)} %all-gather.23.cloned.1.call-done), kind=kOutput, calls=%fused_computation | convolution fusion | flops 11324620800 | bytes 12943360 | tf_op jit(solution)/shard_map/dot_general | solution.py:40
  65.3 1.6 copy-done.16
  66.9 1.1 fusion.68
  68.7 1.4 copy.107
  70.2 1.4 copy.102
  71.5 2.0 copy.103
  73.5 1.0 copy.104
  74.5 1.0 copy.105
  76.9 1.5 fusion.5
  78.7 2.0 bitcast_select_fusion.2
  81.0 8.7 %reshape_reshape_squeeze.4 = f32[1440,1280]{1,0:T(8,128)} reshape(f32[1,160,11520]{2,1,0:T(8,128)} %param.9) | data formatting | bytes 14745600 | tf_op jit(solution)/shard_map/reshape;reshape;squeeze | solution.py:39
  89.7 24.0 %all-gather.11.cloned.1.call-done = f32[1280,512]{1,0:T(8,128)} async-done(((f32[160,512]{1,0:T(8,128)}), f32[1280,512]{1,0:T(8,128)}) %all-gather.11.cloned.1.call-update) | async-done | bytes 2621456 | tf_op jit(solution)/shard_map/all_gather | solution.py:68
  113.7 14.8 %convolution_bitcast_fusion.4 = f32[1440,512]{1,0:T(8,128)S(1)} fusion(f32[1280,512]{1,0:T(8,128)} %all-gather.11.cloned.1.call-done, f32[1440,1280]{1,0:T(8,128)} %reshape_reshape_squeeze.4), kind=kOutput, calls=%fused_computation.6 | convolution fusion | flops 11324620800 | bytes 12943360 | tf_op jit(solution)/shard_map/dot_general | solution.py:40
  128.5 2.6 reshape.406
  131.2 12.2 %fusion.67 = (f32[160,1,512]{2,1,0:T(1,128)S(1)}, f32[160,1,512]{2,1,0:T(1,128)S(1)}, f32[160,1,512]{2,1,0:T(1,128)S(1)}, f32[160,1,512]{2,1,0:T(1,128)S(1)}, f3...) fusion(f32[160,9,512]{2,1,0:T(8,128)} %reshape.406), kind=kLoop, calls=%fused_computation.135 | loop fusion | bytes 5898240 | tf_op jit(solution)/shard_map/slice | solution.py:28
  144.2 1.4 copy.121
  145.6 2.2 copy.115
  147.8 2.0 copy.116
  149.8 2.0 copy.117
  151.7 2.0 copy.118
  154.6 0.9 copy.126
  157.4 1.7 fusion.8
  160.1 2.1 fusion.59
  162.2 3.4 collective-permute-start
  165.6 7.6 %collective-permute-done = f32[160,512]{1,0:T(8,128)S(1)} collective-permute-done((f32[160,512]{1,0:T(8,128)}, f32[160,512]{1,0:T(8,128)S(1)}, u32[]{:S(2)}, u32[]{:S(2)}) %collective-permute-start) | collective-permute-done | bytes 327712 | tf_op jit(solution)/shard_map/ppermute | solution.py:14
  173.2 1.8 bitcast_select_fusion.3
  175.5 8.8 %reshape_reshape_squeeze.5 = f32[1440,1280]{1,0:T(8,128)} reshape(f32[1,160,11520]{2,1,0:T(8,128)} %param.8) | data formatting | bytes 14745600 | tf_op jit(solution)/shard_map/reshape;reshape;squeeze | solution.py:39
  191.2 2.8 multiply_select_fusion.1
  194.1 14.8 %all-gather.13.cloned.1.call-done = f32[1280,512]{1,0:T(8,128)} async-done(((f32[160,512]{1,0:T(8,128)}), f32[1280,512]{1,0:T(8,128)}) %all-gather.13.cloned.1.call-update) | async-done | bytes 2621456 | tf_op jit(solution)/shard_map/all_gather | solution.py:63
  208.9 14.8 %convolution_bitcast_fusion.3 = f32[1440,512]{1,0:T(8,128)S(1)} fusion(f32[1280,512]{1,0:T(8,128)} %all-gather.13.cloned.1.call-done, f32[1440,1280]{1,0:T(8,128)} %reshape_reshape_squeeze.5), kind=kOutput, calls=%fused_computation.5 | convolution fusion | flops 11324620800 | bytes 12943360 | tf_op jit(solution)/shard_map/dot_general | solution.py:40
  223.7 2.5 reshape.412
  226.2 12.2 %fusion.66 = (f32[160,1,512]{2,1,0:T(1,128)S(1)}, f32[160,1,512]{2,1,0:T(1,128)S(1)}, f32[160,1,512]{2,1,0:T(1,128)}, f32[160,1,512]{2,1,0:T(1,128)}, f32[160,1,...) fusion(f32[160,9,512]{2,1,0:T(8,128)} %reshape.412), kind=kLoop, calls=%fused_computation.134 | loop fusion | bytes 5898240 | tf_op jit(solution)/shard_map/slice | solution.py:28
  239.6 1.2 copy.139
  241.7 1.2 copy.137
  243.9 1.2 copy.135
  247.3 2.5 multiply_select_fusion.2
  250.0 32.8 %all-gather.17.cloned.1.call-done = f32[1280,512]{1,0:T(8,128)} async-done(((f32[160,512]{1,0:T(8,128)}), f32[1280,512]{1,0:T(8,128)}) %all-gather.17.cloned.1.call-update) | async-done | bytes 2621456 | tf_op jit(solution)/shard_map/all_gather | solution.py:68
  282.8 14.8 %convolution_bitcast_fusion.2 = f32[1440,512]{1,0:T(8,128)S(1)} fusion(f32[1280,512]{1,0:T(8,128)} %all-gather.17.cloned.1.call-done, f32[1440,1280]{1,0:T(8,128)} %reshape_reshape_squeeze.4), kind=kOutput, calls=%fused_computation.4 | convolution fusion | flops 11324620800 | bytes 12943360 | tf_op jit(solution)/shard_map/dot_general | solution.py:40
  297.6 2.5 reshape.428
  300.1 12.2 %fusion.65 = (f32[160,1,512]{2,1,0:T(1,128)}, f32[160,1,512]{2,1,0:T(1,128)S(1)}, f32[160,1,512]{2,1,0:T(1,128)}, f32[160,1,512]{2,1,0:T(1,128)}, f32[160,1,512]...) fusion(f32[160,9,512]{2,1,0:T(8,128)} %reshape.428), kind=kLoop, calls=%fused_computation.133 | loop fusion | bytes 5898240 | tf_op jit(solution)/shard_map/slice | solution.py:28
  313.5 1.2 copy.163
  315.6 1.2 copy.161
  317.7 1.2 copy.159
  321.2 1.8 multiply_select_fusion
  323.0 3.4 collective-permute-start.1
  326.4 7.3 %collective-permute-done.1 = f32[160,512]{1,0:T(8,128)S(1)} collective-permute-done((f32[160,512]{1,0:T(8,128)S(1)}, f32[160,512]{1,0:T(8,128)S(1)}, u32[]{:S(2)}, u32[]{:S(2)}) %collective-permute-start.1) | collective-permute-done | bytes 327712 | tf_op jit(solution)/shard_map/ppermute | solution.py:14
  335.5 33.0 %all-gather.19.cloned.1.call-done = f32[1280,512]{1,0:T(8,128)} async-done(((f32[160,512]{1,0:T(8,128)}), f32[1280,512]{1,0:T(8,128)}) %all-gather.19.cloned.1.call-update) | async-done | bytes 2621456 | tf_op jit(solution)/shard_map/all_gather | solution.py:63
  368.5 14.8 %convolution_bitcast_fusion.1 = f32[1440,512]{1,0:T(8,128)S(1)} fusion(f32[1280,512]{1,0:T(8,128)} %all-gather.19.cloned.1.call-done, f32[1440,1280]{1,0:T(8,128)} %reshape_reshape_squeeze.5), kind=kOutput, calls=%fused_computation.3 | convolution fusion | flops 11324620800 | bytes 12943360 | tf_op jit(solution)/shard_map/dot_general | solution.py:40
  383.3 2.6 reshape.434
  386.0 12.2 %fusion.64 = (f32[160,1,512]{2,1,0:T(1,128)}, f32[160,1,512]{2,1,0:T(1,128)S(1)}, f32[160,1,512]{2,1,0:T(1,128)}, f32[160,1,512]{2,1,0:T(1,128)}, f32[160,1,512]...) fusion(f32[160,9,512]{2,1,0:T(8,128)} %reshape.434), kind=kLoop, calls=%fused_computation.132 | loop fusion | bytes 5898240 | tf_op jit(solution)/shard_map/slice | solution.py:28
  399.4 1.2 copy.177
  401.5 1.2 copy.175
  403.6 1.2 copy.173
  407.0 2.6 fusion.41
  409.7 33.0 %all-gather.21.cloned.1.call-done = f32[1280,512]{1,0:T(8,128)} async-done(((f32[160,512]{1,0:T(8,128)}), f32[1280,512]{1,0:T(8,128)}) %all-gather.21.cloned.1.call-update) | async-done | bytes 2621456 | tf_op jit(solution)/shard_map/all_gather | solution.py:68
  442.6 15.0 %convolution_bitcast_fusion = f32[1440,512]{1,0:T(8,128)S(1)} fusion(f32[1280,512]{1,0:T(8,128)} %all-gather.21.cloned.1.call-done, f32[1440,1280]{1,0:T(8,128)} %reshape_reshape_squeeze.4), kind=kOutput, calls=%fused_computation.2 | convolution fusion | flops 11324620800 | bytes 12943360 | tf_op jit(solution)/shard_map/dot_general | solution.py:40
  457.7 2.6 reshape.440
  460.3 12.3 %fusion.63 = (f32[160,1,512]{2,1,0:T(1,128)S(1)}, f32[160,1,512]{2,1,0:T(1,128)S(1)}, f32[160,1,512]{2,1,0:T(1,128)}, f32[160,1,512]{2,1,0:T(1,128)}, f32[160,1,...) fusion(f32[160,9,512]{2,1,0:T(8,128)} %reshape.440), kind=kLoop, calls=%fused_computation.131 | loop fusion | bytes 5898240 | tf_op jit(solution)/shard_map/slice | solution.py:28
  473.7 1.2 copy.191
  475.9 1.2 copy.189
  478.0 1.2 copy.187
  481.4 2.4 select_bitcast_fusion
  (175 shorter events, 38.3 us)
Async XLA Ops:
  6.5 38.9 %all-gather.23.cloned.1.call-start = ((), (), s32[]{:S(2)}) async-start(), calls=%async_computation.6 | async-start | bytes 2949120 | tf_op jit(solution)/shard_map/all_gather | solution.py:63
  7.3 106.5 %all-gather.11.cloned.1.call-start = ((), (), s32[]{:S(2)}) async-start(), calls=%async_computation | async-start | bytes 2949120 | tf_op jit(solution)/shard_map/all_gather | solution.py:68
  65.3 1.6 copy-start.16
  68.2 7.3 %copy-start = (f32[160,16,32]{0,2,1:T(8,128)}, f32[160,16,32]{0,2,1:T(8,128)S(1)}, u32[]{:S(2)}) copy-start(f32[160,16,32]{0,2,1:T(8,128)S(1)} %pad_slice_fusion.40) | copy-start | bytes 983044
  68.4 7.2 %copy-start.2 = (f32[160,16,32]{0,2,1:T(8,128)}, f32[160,16,32]{0,2,1:T(8,128)S(1)}, u32[]{:S(2)}) copy-start(f32[160,16,32]{0,2,1:T(8,128)S(1)} %pad_slice_fusion.41) | copy-start | bytes 983044
  68.7 7.9 %copy-start.4 = (f32[160,16,32]{0,2,1:T(8,128)}, f32[160,16,32]{0,2,1:T(8,128)S(1)}, u32[]{:S(2)}) copy-start(f32[160,16,32]{0,2,1:T(8,128)S(1)} %pad_slice_fusion.42) | copy-start | bytes 983044
  70.2 6.6 %copy-start.6 = (f32[160,16,32]{0,2,1:T(8,128)}, f32[160,16,32]{0,2,1:T(8,128)S(1)}, u32[]{:S(2)}) copy-start(f32[160,16,32]{0,2,1:T(8,128)S(1)} %pad_slice_fusion.43) | copy-start | bytes 983044
  75.7 3.0 copy-start.21
  76.6 2.1 copy-start.30
  80.7 128.2 %all-gather.13.cloned.1.call-start = ((), (), s32[]{:S(2)}) async-start(), calls=%async_computation.1 | async-start | bytes 2949120 | tf_op jit(solution)/shard_map/all_gather | solution.py:63
  143.6 10.1 %copy-start.8 = (f32[160,16,32]{0,2,1:T(8,128)}, f32[160,16,32]{0,2,1:T(8,128)S(1)}, u32[]{:S(2)}) copy-start(f32[160,16,32]{0,2,1:T(8,128)S(1)} %pad_slice_fusion.32) | copy-start | bytes 983044
  143.9 10.7 %copy-start.10 = (f32[160,16,32]{0,2,1:T(8,128)}, f32[160,16,32]{0,2,1:T(8,128)S(1)}, u32[]{:S(2)}) copy-start(f32[160,16,32]{0,2,1:T(8,128)S(1)} %pad_slice_fusion.33) | copy-start | bytes 983044
  144.2 11.4 %copy-start.12 = (f32[160,16,32]{0,2,1:T(8,128)}, f32[160,16,32]{0,2,1:T(8,128)S(1)}, u32[]{:S(2)}) copy-start(f32[160,16,32]{0,2,1:T(8,128)S(1)} %pad_slice_fusion.34) | copy-start | bytes 983044
  145.6 10.9 %copy-start.14 = (f32[160,16,32]{0,2,1:T(8,128)}, f32[160,16,32]{0,2,1:T(8,128)S(1)}, u32[]{:S(2)}) copy-start(f32[160,16,32]{0,2,1:T(8,128)S(1)} %pad_slice_fusion.35) | copy-start | bytes 983044
  154.6 5.4 %copy-start.17 = (f32[1,160,512]{2,1,0:T(8,128)S(1)}, f32[1,160,512]{2,1,0:T(8,128)}, u32[]{:S(2)}) copy-start(f32[1,160,512]{2,1,0:T(8,128)} %param.5) | copy-start | bytes 983044
  155.6 4.5 copy-start.24
  156.5 3.6 copy-start.27
  156.5 3.6 copy-start.28
  157.4 2.6 copy-start.29
  162.2 11.0 %collective-permute-start = (f32[160,512]{1,0:T(8,128)}, f32[160,512]{1,0:T(8,128)S(1)}, u32[]{:S(2)}, u32[]{:S(2)}) collective-permute-start(f32[160,512]{1,0:T(8,128)} %fusion.59), channel_id=1, source_target_pairs={{0,8},{8,16},{16,24},{1,9},{9,17},{17,25},{2,10},{10,18},{18,26},{... | collective-permute-start | bytes 983048 | tf_op jit(solution)/shard_map/ppermute | solution.py:14
  175.0 9.3 %copy-start.1 = (f32[160,16,32]{0,2,1:T(8,128)S(1)}, f32[160,16,32]{0,2,1:T(8,128)}, u32[]{:S(2)}) copy-start(f32[160,16,32]{0,2,1:T(8,128)} %copy-done) | copy-start | bytes 983044
  175.0 10.2 %copy-start.3 = (f32[160,16,32]{0,2,1:T(8,128)S(1)}, f32[160,16,32]{0,2,1:T(8,128)}, u32[]{:S(2)}) copy-start(f32[160,16,32]{0,2,1:T(8,128)} %copy-done.2) | copy-start | bytes 983044
  175.0 11.1 %copy-start.5 = (f32[160,16,32]{0,2,1:T(8,128)S(1)}, f32[160,16,32]{0,2,1:T(8,128)}, u32[]{:S(2)}) copy-start(f32[160,16,32]{0,2,1:T(8,128)} %copy-done.4) | copy-start | bytes 983044
  175.0 12.0 %copy-start.7 = (f32[160,16,32]{0,2,1:T(8,128)S(1)}, f32[160,16,32]{0,2,1:T(8,128)}, u32[]{:S(2)}) copy-start(f32[160,16,32]{0,2,1:T(8,128)} %copy-done.6) | copy-start | bytes 983044
  175.0 72.2 %all-gather.15.cloned.1.call-start = ((), (), s32[]{:S(2)}) async-start(), calls=%async_computation.2 | async-start | bytes 1638400 | tf_op jit(solution)/shard_map/all_gather | solution.py:75
  185.2 3.7 copy-start.9
  186.1 3.6 copy-start.11
  187.0 3.6 copy-start.13
  187.9 2.9 copy-start.15
  188.8 2.4 copy-start.18
  189.7 1.4 copy-start.23
  194.0 88.7 %all-gather.17.cloned.1.call-start = ((), (), s32[]{:S(2)}) async-start(), calls=%async_computation.3 | async-start | bytes 2949120 | tf_op jit(solution)/shard_map/all_gather | solution.py:68
  246.2 1.1 copy-start.22
  249.8 118.7 %all-gather.19.cloned.1.call-start = ((), (), s32[]{:S(2)}) async-start(), calls=%async_computation.4 | async-start | bytes 2949120 | tf_op jit(solution)/shard_map/all_gather | solution.py:63
  320.1 1.1 copy-start.19
  321.0 12.7 %copy-start.31 = (f32[2,160,512]{2,1,0:T(8,128)S(1)}, f32[2,160,512]{2,1,0:T(8,128)}, u32[]{:S(2)}) copy-start(f32[2,160,512]{2,1,0:T(8,128)} %param.7) | copy-start | bytes 1966084
  323.0 11.6 %copy-start.26 = (f32[160,512]{1,0:T(8,128)}, f32[160,512]{1,0:T(8,128)S(1)}, u32[]{:S(2)}) copy-start(f32[160,512]{1,0:T(8,128)S(1)} %multiply_select_fusion) | copy-start | bytes 983044
  323.0 10.7 %collective-permute-start.1 = (f32[160,512]{1,0:T(8,128)S(1)}, f32[160,512]{1,0:T(8,128)S(1)}, u32[]{:S(2)}, u32[]{:S(2)}) collective-permute-start(f32[160,512]{1,0:T(8,128)S(1)} %multiply_select_fusion), channel_id=1, source_target_pairs={{0,8},{8,16},{16,24},{1,9},{9,17},{17,25},{2,10},{10,18},{18,26},{... | collective-permute-start | bytes 983048 | tf_op jit(solution)/shard_map/ppermute | solution.py:14
  334.5 72.5 %all-gather.25.cloned.1.call-start = ((), (), s32[]{:S(2)}) async-start(), calls=%async_computation.7 | async-start | bytes 1638400 | tf_op jit(solution)/shard_map/all_gather | solution.py:75
  335.3 107.4 %all-gather.21.cloned.1.call-start = ((), (), s32[]{:S(2)}) async-start(), calls=%async_computation.5 | async-start | bytes 2949120 | tf_op jit(solution)/shard_map/all_gather | solution.py:68
  406.0 1.1 copy-start.25
  480.4 1.0 copy-start.20
Sparse Core Ops, SparseCore 0:
  9.0 36.4 all-gather.22
  80.8 32.8 all-gather.10
  175.1 33.7 all-gather.12
  210.6 27.7 all-gather.14
  249.9 32.8 all-gather.16
  334.6 33.8 all-gather.18
  370.3 27.7 all-gather.24
  409.8 32.8 all-gather.20
where the time goes:
time: 501 us; the launch traced here: 491 us
  waiting for transfers between devices  183 us (37%)
  local copies, waits for them, and re-layouts  168 us (34%)
  matrix products  94.1 us (19%)
  other arithmetic  22.9 us (5%)
  between operations  14.8 us (3%)
  starting transfers between devices  8.06 us (2%)
    slice x54, local copies, waits for them, and re-layouts, place_taps(): total = total + tap_shift(parts[:, 3 * (dy + 1) + (dx + 1)], dy, dx)  97.6 us
    dot_general x6, matrix products, add_piece(): jnp.dot(columns, piece, precision=lax.Precision.HIGHEST, preferred_elemen...  94.1 us
    all_gather x3, waiting for transfers between devices, body(): lax.all_gather(operand, 'chan', axis=0, tiled=True)  89.8 us
    all_gather x3, waiting for transfers between devices, body(): lax.all_gather(field, 'chan', axis=0, tiled=True)  76.7 us
    reshape x32, local copies, waits for them, and re-layouts, tap_shift(): return moved.reshape(field.shape)  25.4 us
    another operation x2, local copies, waits for them, and re-layouts, add_piece(): columns = columns.reshape(out_rows * 9, piece.shape[0])  17.5 us
    ppermute x2, waiting for transfers between devices, passed_along(): return lax.ppermute(array, axis, pairs)  15 us
  transfers between devices with their start and end apart: 10, of which 8 were waited for; matrix products, arithmetic and copies ran while one was open for 23% of the time, Pallas kernels for 0%

commit v1 on v0

v1 whole, which is shorter than its diff:
```python
import functools

import jax
import jax.numpy as jnp
from jax import lax
from jax.experimental import pallas as pl
from jax.experimental.pallas import tpu as pltpu
from jax.sharding import PartitionSpec as P

ROWS = 16
COLS = 32
MESH = pl.DeviceIdType.MESH


def silu(v):
    return v / (1.0 + jnp.exp(-v))


def block_of(rows):
    for size in (32, 40, 16):
        if rows % size == 0:
            return size
    return 8


def kernel(
    segments, n, ticks,
    resident, held_skip, fresh, weights, out_ref,
    wv, g, operand, acc, conv_first, passed_out,
    w_sem, recv_sem, send_sem, pass_send, pass_recv,
):
    seg = lax.axis_index("segment")
    me = lax.axis_index("chan")
    place = me // 2
    core = me % 2
    partner = me + 1 - 2 * core
    length = n // 2
    half = segments // 2
    encoder = seg < half
    rows, positions = resident.shape
    width = 2 * rows
    blk = block_of(rows)

    def load(conv, q):
        return pltpu.make_async_copy(weights.at[conv, q], wv.at[conv, q], w_sem.at[conv, q])

    def start_loads(conv):
        def one(q, _):
            load(conv, q).start()
            return 0
        lax.fori_loop(0, length, one, 0)

    start_loads(0)
    start_loads(1)

    barrier = pltpu.get_barrier_semaphore()

    def greet(cond, segment, chan):
        @pl.when(cond)
        def _():
            pl.semaphore_signal(barrier, inc=1, device_id=(segment, chan), device_id_type=MESH)
        return jnp.where(cond, 1, 0)

    greeted = greet(place > 0, seg, jnp.maximum(me - 2, 0))
    greeted += greet(place < length - 1, seg, jnp.minimum(me + 2, n - 1))
    greeted += greet(place >= 0, seg, partner)
    greeted += greet(seg > 0, jnp.maximum(seg - 1, 0), me)
    greeted += greet(seg < segments - 1, jnp.minimum(seg + 1, segments - 1), me)
    greeted += greet(seg >= 0, segments - 1 - seg, me)
    pl.semaphore_wait(barrier, greeted)

    def hop(k, j, way):
        target = (jnp.maximum(me - 2, 0), jnp.minimum(me + 2, n - 1), partner)[way]
        return pltpu.make_async_remote_copy(
            src_ref=g.at[k, j],
            dst_ref=g.at[k, j],
            send_sem=send_sem.at[way, j],
            recv_sem=recv_sem.at[k, j],
            device_id=(seg, target),
            device_id_type=MESH,
        )

    def give(t, kind):
        target = (jnp.minimum(seg + 1, segments - 1), segments - 1 - seg)[kind]
        return pltpu.make_async_remote_copy(
            src_ref=passed_out.at[t],
            dst_ref=g.at[2 * (t + 1) + kind, me],
            send_sem=pass_send.at[t, kind],
            recv_sem=pass_recv.at[t, kind],
            device_id=(target, me),
            device_id_type=MESH,
        )

    def multiply(k, conv, q, first):
        for i in range(2):
            part = g[k, 2 * q + i]
            high = part.astype(jnp.bfloat16)
            low = (part - high.astype(jnp.float32)).astype(jnp.bfloat16)
            operand[i * rows : (i + 1) * rows] = high
            operand[width + i * rows : width + (i + 1) * rows] = high
            operand[2 * width + i * rows : 2 * width + (i + 1) * rows] = low

        def group(m, _):
            product = jnp.dot(
                wv[conv, q, m], operand[...], preferred_element_type=jnp.float32
            )
            if first:
                acc[m] = product
            else:
                acc[m] += product
            return 0
        lax.fori_loop(0, 3, group, 0)

    def gather_and_multiply(k, conv):
        @pl.when(place < length - 1)
        def _():
            hop(k, me, 1).start()

        @pl.when(place > 0)
        def _():
            hop(k, me, 0).start()

        hop(k, me, 2).start()
        hop(k, partner, 2).wait_recv()
        if k < 2:
            load(conv, place).wait()
        multiply(k, conv, place, True)

        def step(d, _):
            for side in range(2):
                q = place - d if side == 0 else place + d
                there = q >= 0 if side == 0 else q < length
                onward = place < length - 1 if side == 0 else place > 0
                mine = 2 * q + core

                @pl.when(there)
                def _():
                    hop(k, mine, 2).wait_recv()

                    @pl.when(onward)
                    def _():
                        hop(k, mine, 1 - side).start()
                    hop(k, mine, 2).start()

            def one(side, _):
                q = place - d + 2 * d * side

                @pl.when((q >= 0) & (q < length))
                def _():
                    hop(k, 2 * q + 1 - core, 2).wait_recv()
                    if k < 2:
                        load(conv, q).wait()
                    multiply(k, conv, q, False)
                return 0
            lax.fori_loop(0, 2, one, 0)
            return 0
        lax.fori_loop(1, length, step, 0)

        def drain(q, _):
            j = 2 * q + core
            hop(k, j, 2).wait_send()

            @pl.when((q <= place) & (place < length - 1))
            def _():
                hop(k, j, 1).wait_send()

            @pl.when((q >= place) & (place > 0))
            def _():
                hop(k, j, 0).wait_send()
            return 0
        lax.fori_loop(0, length, drain, 0)

    spot = lax.broadcasted_iota(jnp.int32, (blk, positions), 1)
    column = spot % COLS

    def placed(start):
        total = None
        for dx in (-1, 0, 1):
            column_sum = None
            for dy in (-1, 0, 1):
                part = acc[dy + 1, pl.ds(pl.multiple_of((dx + 1) * rows + start, 8), blk), :]
                if dy:
                    part = pltpu.roll(part, (-dy * COLS) % positions, 1)
                    source = spot + dy * COLS
                    part = jnp.where((source >= 0) & (source < positions), part, 0.0)
                column_sum = part if column_sum is None else column_sum + part
            if dx:
                column_sum = pltpu.roll(column_sum, (-dx) % positions, 1)
                source = column + dx
                column_sum = jnp.where((source >= 0) & (source < COLS), column_sum, 0.0)
            total = column_sum if total is None else total + column_sum
        return total

    def over_rows(action):
        def one(i, _):
            start = pl.multiple_of(i * blk, 8)
            action(start, pl.ds(start, blk))
            return 0
        lax.fori_loop(0, rows // blk, one, 0)

    g[0, me] = resident[...]

    @pl.when(jnp.logical_not(encoder))
    def _():
        g[1, me] = held_skip[...]

    for t in range(ticks):
        k = 2 * t
        if t:
            @pl.when(seg > 0)
            def _():
                give(t - 1, 0).wait_recv()

            @pl.when(seg == 0)
            def _():
                g[k, me] = fresh[t - 1]

        gather_and_multiply(k, 0)

        def after_first(start, rows_of):
            value = placed(start)
            conv_first[rows_of, :] = value

            @pl.when(encoder)
            def _():
                g[k + 1, me, rows_of, :] = silu(value)
        over_rows(after_first)
        if t:
            @pl.when(jnp.logical_not(encoder))
            def _():
                give(t - 1, 1).wait_recv()

        gather_and_multiply(k + 1, 1)

        def after_second(start, rows_of):
            value = placed(start)

            @pl.when(encoder)
            def _():
                passed_out[t, rows_of, :] = g[k, me, rows_of, :] + value

            @pl.when(jnp.logical_not(encoder))
            def _():
                passed_out[t, rows_of, :] = silu(conv_first[rows_of, :] + value)
        over_rows(after_second)

        if t < ticks - 1:
            @pl.when(seg < segments - 1)
            def _():
                give(t, 0).start()

            @pl.when(encoder)
            def _():
                give(t, 1).start()

    for t in range(ticks - 1):
        @pl.when(seg < segments - 1)
        def _():
            give(t, 0).wait_send()

        @pl.when(encoder)
        def _():
            give(t, 1).wait_send()
    out_ref[...] = passed_out[ticks - 1]


def split_weight(weight, length):
    rows = weight.shape[0]
    width = weight.shape[1] // 9 // length
    high = lax.reduce_precision(weight, 8, 7)
    low = weight - high
    high, low = high.astype(jnp.bfloat16), low.astype(jnp.bfloat16)

    def by_piece(part):
        part = part.reshape(rows, 3, 3, length, width)
        return part.transpose(3, 1, 2, 0, 4).reshape(length, 3, 3 * rows, width)

    high, low = by_piece(high), by_piece(low)
    return jnp.concatenate([high, low, high], axis=-1)


def body(segments, n, resident, held_skip, fresh, first_weight, second_weight):
    ticks = fresh.shape[0] + 1
    rows, positions = resident.shape[1:]
    length = n // 2
    width = 2 * rows
    weights = jnp.stack([split_weight(first_weight[0], length), split_weight(second_weight[0], length)])
    vmem = pl.BlockSpec(memory_space=pltpu.VMEM)
    out = pl.pallas_call(
        functools.partial(kernel, segments, n, ticks),
        out_shape=jax.ShapeDtypeStruct((rows, positions), jnp.float32),
        in_specs=[vmem, vmem, vmem, pl.BlockSpec(memory_space=pl.ANY)],
        out_specs=vmem,
        scratch_shapes=[
            pltpu.VMEM((2, length, 3, 3 * rows, 3 * width), jnp.bfloat16),
            pltpu.VMEM((2 * ticks, n, rows, positions), jnp.float32),
            pltpu.VMEM((3 * width, positions), jnp.bfloat16),
            pltpu.VMEM((3, 3 * rows, positions), jnp.float32),
            pltpu.VMEM((rows, positions), jnp.float32),
            pltpu.VMEM((ticks, rows, positions), jnp.float32),
            pltpu.SemaphoreType.DMA((2, length)),
            pltpu.SemaphoreType.DMA((2 * ticks, n)),
            pltpu.SemaphoreType.DMA((3, n)),
            pltpu.SemaphoreType.DMA((ticks - 1, 2)),
            pltpu.SemaphoreType.DMA((ticks - 1, 2)),
        ],
        compiler_params=pltpu.CompilerParams(
            collective_id=0, has_side_effects=True, vmem_limit_bytes=60 * 1024 * 1024
        ),
    )(resident[0], held_skip[0], fresh, weights)
    return out[None]


def solution(mesh):
    return jax.shard_map(
        functools.partial(body, mesh.shape["segment"], mesh.shape["chan"]),
        mesh=mesh,
        in_specs=(
            P("segment", "chan", None),
            P("segment", "chan", None),
            P(None, "chan", None),
            P("segment", "chan", None),
            P("segment", "chan", None),
        ),
        out_specs=P("segment", "chan", None),
        check_vma=False,
    )
```

time: 501 us -> 274 us (0.55)
  the two profiles are of different devices: /device:TPU:0 before, /device:TPU:5 now
where the time goes in v1:
time: 274 us; the launch traced here: 273 us
  Pallas kernels  209 us (76%)
  other arithmetic  41.2 us (15%)
  local copies, waits for them, and re-layouts  23.3 us (9%)
    pallas_call x1, Pallas kernels, body(): pl.pallas_call(functools.partial(kernel, segments, n, ticks), out_shape=j...  209 us
    another operation x2, other arithmetic, body(): jnp.stack([split_weight(first_weight[0], length), split_weight(second_wei...  24.2 us
    convert_element_type x2, other arithmetic, split_weight(): high, low = (high.astype(jnp.bfloat16), low.astype(jnp.bfloat16))  17 us
    squeeze x1, local copies, waits for them, and re-layouts, body(): second_weight[0]  10.8 us
    squeeze x1, local copies, waits for them, and re-layouts, body(): first_weight[0]  10.8 us

profile of v1, /device:TPU:5, one launch (start us, length us, event | category | flops | bytes accessed | tf_op | source)
XLA Modules:
  0.0 273.3 jit_solution(18248289080493975452)
XLA Ops:
  0.0 10.8 %squeeze.14 = f32[160,3,3,4,320]{4,3,2,1,0:T(4,128)} reshape(f32[1,160,11520]{2,1,0:T(8,128)} %param.8) | data formatting | bytes 14745600 | tf_op jit(solution)/shard_map/squeeze | solution.py:287
  10.8 8.4 %fusion = (bf16[160,3,3,4,320]{4,0,2,1,3:T(8,128)(2,1)}, bf16[160,3,3,4,320]{4,0,2,1,3:T(8,128)(2,1)}) fusion(f32[160,3,3,4,320]{4,3,2,1,0:T(4,128)} %squeeze.14), kind=kLoop, calls=%fused_computation.7 | loop fusion | flops 7372800 | bytes 14745600 | tf_op jit(solution)/shard_map/convert_element_type | solution.py:272
  19.1 0.0 slice-start
  19.2 10.8 %squeeze.15 = f32[160,3,3,4,320]{4,3,2,1,0:T(4,128)} reshape(f32[1,160,11520]{2,1,0:T(8,128)} %param.9) | data formatting | bytes 14745600 | tf_op jit(solution)/shard_map/squeeze | solution.py:287
  30.0 0.0 slice-start.1
  30.0 8.6 %fusion.1 = (bf16[160,3,3,4,320]{4,0,2,1,3:T(8,128)(2,1)}, bf16[160,3,3,4,320]{4,0,2,1,3:T(8,128)(2,1)}) fusion(f32[160,3,3,4,320]{4,3,2,1,0:T(4,128)} %squeeze.15), kind=kLoop, calls=%fused_computation.8 | loop fusion | flops 7372800 | bytes 14745600 | tf_op jit(solution)/shard_map/convert_element_type | solution.py:272
  38.6 0.0 slice-done
  38.6 0.0 slice-done.1
  38.6 14.5 %maximum_bitcast_fusion = (bf16[1,4,3,480,960]{4,3,2,1,0:T(8,128)(2,1)S(1)}, bf16[1,4,3,480,960]{4,3,2,1,0:T(8,128)(2,1)S(1)}) fusion(bf16[4,3,480,320]{3,2,1,0:T(8,128)(2,1)} %bitcast.22, bf16[4,3,480,320]{3,2,1,0:T(8,128)(2,1)S(1)} %bitcast.21, bf16[4,3,480,320]{3,2,1,0:T(8,128)(2,1)} %bitcast.24, bf16[4,3,480,320]{3,2,1,0:T(8,128)(2,1)} %bitcast.23), kind=kLoop, calls=%fused_computation.5 | loop fusion | flops 66355200 | bytes 36864000 | tf_op jit(solution)/shard_map/stack | solution.py:287
  53.1 9.7 %pad_maximum_fusion.weights = bf16[2,4,3,480,960]{4,3,2,1,0:T(8,128)(2,1)} fusion(bf16[1,4,3,480,960]{4,3,2,1,0:T(8,128)(2,1)S(1)} %get-tuple-element.10, bf16[1,4,3,480,960]{4,3,2,1,0:T(8,128)(2,1)S(1)} %get-tuple-element.9), kind=kLoop, calls=%fused_computation | loop fusion | flops 11059200 | bytes 44236800 | tf_op jit(solution)/shard_map/stack | solution.py:287
  62.8 208.7 %shard_map.55 = f32[160,512]{1,0:T(8,128)} custom-call(f32[160,512]{1,0:T(8,128)} %bitcast.26, f32[160,512]{1,0:T(8,128)} %bitcast.27, f32[2,160,512]{2,1,0:T(8,128)} %fresh.1, bf16[2,4,3,480,960]{4,3,2,1,0:T(8,128)(2,1)} %pad_maximum_fusion.weights), custom_call_target="tpu_custom_call" | custom-call | tf_op jit(solution)/shard_map/pallas_call | solution.py:289
  271.6 1.7 copy.15
  (1 shorter events, 0.0 us)
Async XLA Ops:
  19.1 19.5 %slice-start = ((s8[4423680]{0:T(1024)(128)(4,1)}), s8[229376]{0:T(1024)(128)(4,1)S(1)}, s32[]{:S(2)}) async-start(s8[4423680]{0:T(1024)(128)(4,1)} %bitcast.19), calls=%async_computation | async-start | bytes 458752
  30.0 8.6 %slice-start.1 = ((s8[4423680]{0:T(1024)(128)(4,1)}), s8[4194304]{0:T(1024)(128)(4,1)S(1)}, s32[]{:S(2)}) async-start(s8[4423680]{0:T(1024)(128)(4,1)} %bitcast.19), calls=%async_computation.1 | async-start | bytes 8388608

commit v2 on v1

v2 whole, which is shorter than its diff:
```python
import functools

import jax
import jax.numpy as jnp
from jax import lax
from jax.experimental import pallas as pl
from jax.experimental.pallas import tpu as pltpu
from jax.sharding import PartitionSpec as P

ROWS = 16
COLS = 32
MESH = pl.DeviceIdType.MESH


def silu(v):
    return v / (1.0 + jnp.exp(-v))


def block_of(rows):
    for size in (32, 40, 16):
        if rows % size == 0:
            return size
    return 8


HALVES = 2


def kernel(
    segments, n, ticks,
    resident, held_skip, fresh, first_weight, second_weight, out_ref,
    stage, wv, g, operand, acc, conv_first, passed_out,
    w_sem, recv_sem, send_sem, pass_send, pass_recv,
):
    seg = lax.axis_index("segment")
    me = lax.axis_index("chan")
    place = me // 2
    core = me % 2
    partner = me + 1 - 2 * core
    length = n // 2
    half = segments // 2
    encoder = seg < half
    shares_input = seg == half
    rows, positions = resident.shape
    part_positions = positions // HALVES
    width = 2 * rows
    channels = length * width
    blk = block_of(rows)
    split_blk = 32 if rows % 32 == 0 else rows

    def load(conv, tap):
        source = (first_weight, second_weight)[conv]
        columns = pl.ds(pl.multiple_of(tap * channels, 128), channels)
        return pltpu.make_async_copy(source.at[0, :, columns], stage.at[tap], w_sem.at[tap])

    def start_loads(conv):
        def one(tap, _):
            load(conv, tap).start()
            return 0
        lax.fori_loop(0, 9, one, 0)

    def split_weights(conv):
        def three_taps(y, _):
            for x in range(3):
                tap = 3 * y + x
                load(conv, tap).wait()

                def some_rows(i, _):
                    start = i * split_blk
                    if split_blk != rows:
                        start = pl.multiple_of(start, 16)
                    for q in range(length):
                        value = stage[tap, pl.ds(start, split_blk), q * width : (q + 1) * width]
                        high = value.astype(jnp.bfloat16)
                        low = (value - high.astype(jnp.float32)).astype(jnp.bfloat16)
                        spot = pl.ds(x * rows + start, split_blk)
                        if split_blk != rows:
                            spot = pl.ds(pl.multiple_of(x * rows + start, 16), split_blk)
                        wv[conv, q, y, spot, 0:width] = high
                        wv[conv, q, y, spot, width : 2 * width] = low
                        wv[conv, q, y, spot, 2 * width : 3 * width] = high
                    return 0
                if split_blk == rows:
                    some_rows(0, 0)
                else:
                    lax.fori_loop(0, rows // split_blk, some_rows, 0)
            return 0
        lax.fori_loop(0, 3, three_taps, 0)

    start_loads(0)

    barrier = pltpu.get_barrier_semaphore()

    def greet(cond, segment, chan):
        @pl.when(cond)
        def _():
            pl.semaphore_signal(barrier, inc=1, device_id=(segment, chan), device_id_type=MESH)
        return jnp.where(cond, 1, 0)

    greeted = greet(place > 0, seg, jnp.maximum(me - 2, 0))
    greeted += greet(place < length - 1, seg, jnp.minimum(me + 2, n - 1))
    greeted += greet(place >= 0, seg, partner)
    greeted += greet(seg > 0, jnp.maximum(seg - 1, 0), me)
    greeted += greet(seg < segments - 1, jnp.minimum(seg + 1, segments - 1), me)
    greeted += greet(seg >= 0, segments - 1 - seg, me)
    pl.semaphore_wait(barrier, greeted)

    def hop(k, j, h, way):
        target = (jnp.maximum(me - 2, 0), jnp.minimum(me + 2, n - 1), partner)[way]
        return pltpu.make_async_remote_copy(
            src_ref=g.at[k, j, h],
            dst_ref=g.at[k, j, h],
            send_sem=send_sem.at[way, j, h],
            recv_sem=recv_sem.at[k, j, h],
            device_id=(seg, target),
            device_id_type=MESH,
        )

    def give(t, kind, h):
        target = (jnp.minimum(seg + 1, segments - 1), segments - 1 - seg)[kind]
        return pltpu.make_async_remote_copy(
            src_ref=passed_out.at[t, h],
            dst_ref=g.at[2 * (t + 1) + kind, me, h],
            send_sem=pass_send.at[t, kind, h],
            recv_sem=pass_recv.at[t, kind, h],
            device_id=(target, me),
            device_id_type=MESH,
        )

    def multiply(k, conv, q, h, first):
        for i in range(2):
            part = g[k, 2 * q + i, h]
            high = part.astype(jnp.bfloat16)
            low = (part - high.astype(jnp.float32)).astype(jnp.bfloat16)
            operand[i * rows : (i + 1) * rows] = high
            operand[width + i * rows : width + (i + 1) * rows] = high
            operand[2 * width + i * rows : 2 * width + (i + 1) * rows] = low

        def group(m, _):
            product = jnp.dot(
                wv[conv, q, m], operand[...], preferred_element_type=jnp.float32
            )
            if first:
                acc[h, m] = product
            else:
                acc[h, m] += product
            return 0
        lax.fori_loop(0, 3, group, 0)

    def gather_and_multiply(k, conv, ready):
        for h in range(HALVES):
            ready(h)

            @pl.when(place < length - 1)
            def _():
                hop(k, me, h, 1).start()

            @pl.when(place > 0)
            def _():
                hop(k, me, h, 0).start()

            hop(k, me, h, 2).start()

        if k < 2:
            split_weights(conv)
            if conv == 0:
                start_loads(1)

        def own(h, _):
            hop(k, partner, h, 2).wait_recv()
            multiply(k, conv, place, h, True)
            return 0
        lax.fori_loop(0, HALVES, own, 0)

        def step(u, _):
            d = u // HALVES
            h = u % HALVES
            for side in range(2):
                q = place - d if side == 0 else place + d
                there = q >= 0 if side == 0 else q < length
                onward = place < length - 1 if side == 0 else place > 0
                mine = 2 * q + core

                @pl.when(there)
                def _():
                    hop(k, mine, h, 2).wait_recv()

                    @pl.when(onward)
                    def _():
                        hop(k, mine, h, 1 - side).start()
                    hop(k, mine, h, 2).start()

            def one(side, _):
                q = place - d + 2 * d * side

                @pl.when((q >= 0) & (q < length))
                def _():
                    hop(k, 2 * q + 1 - core, h, 2).wait_recv()
                    multiply(k, conv, q, h, False)
                return 0
            lax.fori_loop(0, 2, one, 0)
            return 0
        lax.fori_loop(HALVES, length * HALVES, step, 0)

        def drain(u, _):
            q = u // HALVES
            h = u % HALVES
            j = 2 * q + core
            hop(k, j, h, 2).wait_send()

            @pl.when((q <= place) & (place < length - 1))
            def _():
                hop(k, j, h, 1).wait_send()

            @pl.when((q >= place) & (place > 0))
            def _():
                hop(k, j, h, 0).wait_send()
            return 0
        lax.fori_loop(0, length * HALVES, drain, 0)

    def multiply_held(k, conv):
        for h in range(HALVES):
            multiply(k, conv, 0, h, True)

        def one(u, _):
            multiply(k, conv, u // HALVES, u % HALVES, False)
            return 0
        lax.fori_loop(HALVES, length * HALVES, one, 0)

    spot = lax.broadcasted_iota(jnp.int32, (blk, positions), 1)
    column = spot % COLS

    def placed(start):
        total = None
        for dx in (-1, 0, 1):
            column_sum = None
            for dy in (-1, 0, 1):
                at = pl.ds(pl.multiple_of((dx + 1) * rows + start, 8), blk)
                part = jnp.concatenate([acc[h, dy + 1, at, :] for h in range(HALVES)], axis=1)
                if dy:
                    part = pltpu.roll(part, (-dy * COLS) % positions, 1)
                    source = spot + dy * COLS
                    part = jnp.where((source >= 0) & (source < positions), part, 0.0)
                column_sum = part if column_sum is None else column_sum + part
            if dx:
                column_sum = pltpu.roll(column_sum, (-dx) % positions, 1)
                source = column + dx
                column_sum = jnp.where((source >= 0) & (source < COLS), column_sum, 0.0)
            total = column_sum if total is None else total + column_sum
        return total

    def over_rows(action):
        def one(i, _):
            start = pl.multiple_of(i * blk, 8)
            action(start, pl.ds(start, blk))
            return 0
        lax.fori_loop(0, rows // blk, one, 0)

    def halves_of(value):
        return [value[:, h * part_positions : (h + 1) * part_positions] for h in range(HALVES)]

    def nothing(h):
        pass

    for h in range(HALVES):
        cut = slice(h * part_positions, (h + 1) * part_positions)
        g[0, me, h] = resident[:, cut]

        @pl.when(jnp.logical_not(encoder))
        def _():
            g[1, me, h] = held_skip[:, cut]

    for t in range(ticks):
        k = 2 * t

        def input_ready(h):
            if t == 0:
                return

            @pl.when(seg > 0)
            def _():
                give(t - 1, 0, h).wait_recv()

            @pl.when(seg == 0)
            def _():
                g[k, me, h] = fresh[t - 1, :, h * part_positions : (h + 1) * part_positions]

        gather_and_multiply(k, 0, input_ready)

        def after_first(start, rows_of):
            value = placed(start)
            conv_first[rows_of, :] = value

            @pl.when(encoder)
            def _():
                for h, part in enumerate(halves_of(silu(value))):
                    g[k + 1, me, h, rows_of, :] = part
        over_rows(after_first)

        if t == 0:
            gather_and_multiply(1, 1, nothing)
        else:
            def operand_ready(h):
                @pl.when(jnp.logical_not(encoder))
                def _():
                    give(t - 1, 1, h).wait_recv()

            @pl.when(shares_input)
            def _():
                multiply_held(k, 1)

            @pl.when(jnp.logical_not(shares_input))
            def _():
                gather_and_multiply(k + 1, 1, operand_ready)

        def after_second(start, rows_of):
            value = placed(start)

            @pl.when(encoder)
            def _():
                for h, part in enumerate(halves_of(value)):
                    passed_out[t, h, rows_of, :] = g[k, me, h, rows_of, :] + part

            @pl.when(jnp.logical_not(encoder))
            def _():
                for h, part in enumerate(halves_of(silu(conv_first[rows_of, :] + value))):
                    passed_out[t, h, rows_of, :] = part
        over_rows(after_second)

        if t < ticks - 1:
            @pl.when(seg < segments - 1)
            def _():
                for h in range(HALVES):
                    give(t, 0, h).start()

            @pl.when(seg < half - 1)
            def _():
                for h in range(HALVES):
                    give(t, 1, h).start()

    for t in range(ticks - 1):
        for h in range(HALVES):
            @pl.when(seg < segments - 1)
            def _():
                give(t, 0, h).wait_send()

            @pl.when(seg < half - 1)
            def _():
                give(t, 1, h).wait_send()
    for h in range(HALVES):
        out_ref[:, h * part_positions : (h + 1) * part_positions] = passed_out[ticks - 1, h]


def body(segments, n, resident, held_skip, fresh, first_weight, second_weight):
    ticks = fresh.shape[0] + 1
    rows, positions = resident.shape[1:]
    part_positions = positions // HALVES
    length = n // 2
    width = 2 * rows
    vmem = pl.BlockSpec(memory_space=pltpu.VMEM)
    anywhere = pl.BlockSpec(memory_space=pl.ANY)
    out = pl.pallas_call(
        functools.partial(kernel, segments, n, ticks),
        out_shape=jax.ShapeDtypeStruct((rows, positions), jnp.float32),
        in_specs=[vmem, vmem, vmem, anywhere, anywhere],
        out_specs=vmem,
        scratch_shapes=[
            pltpu.VMEM((9, rows, length * width), jnp.float32),
            pltpu.VMEM((2, length, 3, 3 * rows, 3 * width), jnp.bfloat16),
            pltpu.VMEM((2 * ticks, n, HALVES, rows, part_positions), jnp.float32),
            pltpu.VMEM((3 * width, part_positions), jnp.bfloat16),
            pltpu.VMEM((HALVES, 3, 3 * rows, part_positions), jnp.float32),
            pltpu.VMEM((rows, positions), jnp.float32),
            pltpu.VMEM((ticks, HALVES, rows, part_positions), jnp.float32),
            pltpu.SemaphoreType.DMA((9,)),
            pltpu.SemaphoreType.DMA((2 * ticks, n, HALVES)),
            pltpu.SemaphoreType.DMA((3, n, HALVES)),
            pltpu.SemaphoreType.DMA((ticks - 1, 2, HALVES)),
            pltpu.SemaphoreType.DMA((ticks - 1, 2, HALVES)),
        ],
        compiler_params=pltpu.CompilerParams(
            collective_id=0, has_side_effects=True, vmem_limit_bytes=62 * 1024 * 1024
        ),
    )(resident[0], held_skip[0], fresh, first_weight, second_weight)
    return out[None]


def solution(mesh):
    return jax.shard_map(
        functools.partial(body, mesh.shape["segment"], mesh.shape["chan"]),
        mesh=mesh,
        in_specs=(
            P("segment", "chan", None),
            P("segment", "chan", None),
            P(None, "chan", None),
            P("segment", "chan", None),
            P("segment", "chan", None),
        ),
        out_specs=P("segment", "chan", None),
        check_vma=False,
    )
```

time: 274 us -> 174 us (0.64)
  the two profiles are of different devices: /device:TPU:5 before, /device:TPU:3 now
where the time goes in v2:
time: 174 us; the launch traced here: 173 us
  Pallas kernels  172 us (99%)
    pallas_call x1, Pallas kernels, body(): pl.pallas_call(functools.partial(kernel, segments, n, ticks), out_shape=j...  172 us

profile of v2, /device:TPU:3, one launch (start us, length us, event | category | flops | bytes accessed | tf_op | source)
XLA Modules:
  0.0 173.4 jit_solution(13396428327891387145)
XLA Ops:
  0.0 171.6 %shard_map.55 = f32[160,512]{1,0:T(8,128)} custom-call(f32[160,512]{1,0:T(8,128)} %bitcast.4, f32[160,512]{1,0:T(8,128)} %bitcast.5, f32[2,160,512]{2,1,0:T(8,128)} %fresh.1, f32[1,160,11520]{2,1,0:T(8,128)} %first_weight.1, f32[1,160,11520]{2,1,0:T(8,128)} %second_weight.1), custom_call_target="tpu_custom_call" | custom-call | tf_op jit(solution)/shard_map/pallas_call | solution.py:362
  171.6 1.7 copy.7

commit v3 on v2

v3 whole, which is shorter than its diff:
```python
import functools

import jax
import jax.numpy as jnp
from jax import lax
from jax.experimental import pallas as pl
from jax.experimental.pallas import tpu as pltpu
from jax.sharding import PartitionSpec as P

ROWS = 16
COLS = 32
MESH = pl.DeviceIdType.MESH


def silu(v):
    return v / (1.0 + jnp.exp(-v))


def block_of(rows):
    for size in (32, 40, 16):
        if rows % size == 0:
            return size
    return 8


HALVES = 2
QUARTERS = 4
UNITS = ((0, 1), (1, 1), (2, 2))


def kernel(
    segments, n, ticks,
    resident, held_skip, fresh, first_weight, second_weight, out_ref,
    stage, wv, g, operand, acc, conv_first, passed_out,
    w_sem, recv_sem, send_sem, direct_sem, pass_send, pass_recv,
):
    seg = lax.axis_index("segment")
    me = lax.axis_index("chan")
    place = me // 2
    core = me % 2
    partner = me + 1 - 2 * core
    length = n // 2
    half = segments // 2
    encoder = seg < half
    shares_input = seg == half
    rows, positions = resident.shape
    quarter = positions // QUARTERS
    width = 2 * rows
    channels = length * width
    blk = block_of(rows)
    split_blk = 32 if rows % 32 == 0 else rows

    def load(conv, tap):
        source = (first_weight, second_weight)[conv]
        columns = pl.ds(pl.multiple_of(tap * channels, 128), channels)
        return pltpu.make_async_copy(source.at[0, :, columns], stage.at[tap], w_sem.at[tap])

    def start_loads(conv):
        def one(tap, _):
            load(conv, tap).start()
            return 0
        lax.fori_loop(0, 9, one, 0)

    def split_weights(conv):
        def three_taps(y, _):
            for x in range(3):
                tap = 3 * y + x
                load(conv, tap).wait()

                def some_rows(i, _):
                    start = i * split_blk
                    if split_blk != rows:
                        start = pl.multiple_of(start, 16)
                    for q in range(length):
                        value = stage[tap, pl.ds(start, split_blk), q * width : (q + 1) * width]
                        high = value.astype(jnp.bfloat16)
                        low = (value - high.astype(jnp.float32)).astype(jnp.bfloat16)
                        spot = pl.ds(x * rows + start, split_blk)
                        if split_blk != rows:
                            spot = pl.ds(pl.multiple_of(x * rows + start, 16), split_blk)
                        wv[conv, q, y, spot, 0:width] = high
                        wv[conv, q, y, spot, width : 2 * width] = low
                        wv[conv, q, y, spot, 2 * width : 3 * width] = high
                    return 0
                if split_blk == rows:
                    some_rows(0, 0)
                else:
                    lax.fori_loop(0, rows // split_blk, some_rows, 0)
            return 0
        lax.fori_loop(0, 3, three_taps, 0)

    start_loads(0)

    barrier = pltpu.get_barrier_semaphore()

    def greet(cond, segment, chan):
        @pl.when(cond)
        def _():
            pl.semaphore_signal(barrier, inc=1, device_id=(segment, chan), device_id_type=MESH)
        return jnp.where(cond, 1, 0)

    def greet_line(q, _):
        greet(q != place, seg, 2 * q + core)
        return 0
    lax.fori_loop(0, length, greet_line, 0)
    greeted = length - 1
    greeted += greet(place >= 0, seg, partner)
    greeted += greet(seg > 0, jnp.maximum(seg - 1, 0), me)
    greeted += greet(seg < segments - 1, jnp.minimum(seg + 1, segments - 1), me)
    greeted += greet(seg >= 0, segments - 1 - seg, me)
    pl.semaphore_wait(barrier, greeted)

    def span(unit):
        return pl.ds(*UNITS[unit])

    def hop(k, j, unit, way):
        target = (jnp.maximum(me - 2, 0), jnp.minimum(me + 2, n - 1), partner)[way]
        return pltpu.make_async_remote_copy(
            src_ref=g.at[k, j, span(unit)],
            dst_ref=g.at[k, j, span(unit)],
            send_sem=send_sem.at[k % 2, way, j, unit],
            recv_sem=recv_sem.at[k, j, unit],
            device_id=(seg, target),
            device_id_type=MESH,
        )

    def direct(k, q):
        return pltpu.make_async_remote_copy(
            src_ref=g.at[k, me, span(0)],
            dst_ref=g.at[k, me, span(0)],
            send_sem=direct_sem.at[k % 2, q],
            recv_sem=recv_sem.at[k, me, 0],
            device_id=(seg, 2 * q + core),
            device_id_type=MESH,
        )

    def send_early(k):
        hop(k, me, 0, 2).start()

        def one(q, _):
            @pl.when(q != place)
            def _():
                direct(k, q).start()
            return 0
        lax.fori_loop(0, length, one, 0)

    def give(t, kind, unit):
        target = (jnp.minimum(seg + 1, segments - 1), segments - 1 - seg)[kind]
        return pltpu.make_async_remote_copy(
            src_ref=passed_out.at[t, span(unit)],
            dst_ref=g.at[2 * (t + 1) + kind, me, span(unit)],
            send_sem=pass_send.at[t, kind, unit],
            recv_sem=pass_recv.at[t, kind, unit],
            device_id=(target, me),
            device_id_type=MESH,
        )

    def give_unit(t, unit):
        @pl.when(seg < segments - 1)
        def _():
            give(t, 0, unit).start()

        @pl.when(seg < half - 1)
        def _():
            give(t, 1, unit).start()

    def clear():
        for h in range(HALVES):
            def one(m, _):
                acc[h, m] = jnp.zeros(acc.shape[2:], jnp.float32)
                return 0
            lax.fori_loop(0, 3, one, 0)

    def multiply(k, conv, q, h):
        for i in range(2):
            for c in range(2):
                part = g[k, 2 * q + i, 2 * h + c]
                high = part.astype(jnp.bfloat16)
                low = (part - high.astype(jnp.float32)).astype(jnp.bfloat16)
                cut = slice(c * quarter, (c + 1) * quarter)
                operand[i * rows : (i + 1) * rows, cut] = high
                operand[width + i * rows : width + (i + 1) * rows, cut] = high
                operand[2 * width + i * rows : 2 * width + (i + 1) * rows, cut] = low

        def group(m, _):
            acc[h, m] += jnp.dot(
                wv[conv, q, m], operand[...], preferred_element_type=jnp.float32
            )
            return 0
        lax.fori_loop(0, 3, group, 0)

    def gather_and_multiply(k, conv, ready, early):
        for unit in (1, 2):
            ready(unit)

            @pl.when(place < length - 1)
            def _():
                hop(k, me, unit, 1).start()

            @pl.when(place > 0)
            def _():
                hop(k, me, unit, 0).start()

            hop(k, me, unit, 2).start()

        if k < 2:
            split_weights(conv)
            if conv == 0:
                start_loads(1)
        clear()

        def step(d, h):
            unit = h + 1
            for side in range(2):
                q = place - d if side == 0 else place + d
                there = (d > 0) & (q >= 0 if side == 0 else q < length)
                onward = place < length - 1 if side == 0 else place > 0
                mine = 2 * q + core

                @pl.when(there)
                def _():
                    if h == 0:
                        hop(k, mine, 0, 2).wait_recv()
                        hop(k, mine, 0, 2).start()
                    hop(k, mine, unit, 2).wait_recv()

                    @pl.when(onward)
                    def _():
                        hop(k, mine, unit, 1 - side).start()
                    hop(k, mine, unit, 2).start()

            def one(side, _):
                q = place - d + 2 * d * side

                @pl.when((q >= 0) & (q < length) & ((d > 0) | (side == 0)))
                def _():
                    if h == 0:
                        hop(k, 2 * q + 1 - core, 0, 2).wait_recv()
                    hop(k, 2 * q + 1 - core, unit, 2).wait_recv()
                    multiply(k, conv, q, h)
                return 0
            lax.fori_loop(0, 2, one, 0)

        def both(d, _):
            step(d, 0)
            step(d, 1)
            return 0
        lax.fori_loop(0, length - 1, both, 0)
        step(jnp.int32(length - 1), 0)
        early()
        step(jnp.int32(length - 1), 1)

        def drain(q, _):
            j = 2 * q + core
            hop(k, j, 0, 2).wait_send()

            @pl.when(q != place)
            def _():
                direct(k, q).wait_send()

            for unit in (1, 2):
                hop(k, j, unit, 2).wait_send()

                @pl.when((q <= place) & (place < length - 1))
                def _():
                    hop(k, j, unit, 1).wait_send()

                @pl.when((q >= place) & (place > 0))
                def _():
                    hop(k, j, unit, 0).wait_send()
            return 0
        lax.fori_loop(0, length, drain, 0)

    def multiply_held(k, conv, early):
        clear()
        for h in range(HALVES):
            def one(q, _):
                multiply(k, conv, q, h)
                return 0
            lax.fori_loop(0, length, one, 0)
            if h == 0:
                early()

    def placed(start, halves):
        extent = 2 * quarter * halves
        spot = lax.broadcasted_iota(jnp.int32, (blk, extent), 1)
        column = spot % COLS
        total = None
        for dx in (-1, 0, 1):
            column_sum = None
            for dy in (-1, 0, 1):
                at = pl.ds(pl.multiple_of((dx + 1) * rows + start, 8), blk)
                part = jnp.concatenate([acc[h, dy + 1, at, :] for h in range(halves)], axis=1)
                if dy:
                    part = pltpu.roll(part, (-dy * COLS) % extent, 1)
                    source = spot + dy * COLS
                    part = jnp.where((source >= 0) & (source < extent), part, 0.0)
                column_sum = part if column_sum is None else column_sum + part
            if dx:
                column_sum = pltpu.roll(column_sum, (-dx) % extent, 1)
                source = column + dx
                column_sum = jnp.where((source >= 0) & (source < COLS), column_sum, 0.0)
            total = column_sum if total is None else total + column_sum
        return total

    def over_rows(action):
        def one(i, _):
            start = pl.multiple_of(i * blk, 8)
            action(start, pl.ds(start, blk))
            return 0
        lax.fori_loop(0, rows // blk, one, 0)

    def cut(c):
        return slice(c * quarter, (c + 1) * quarter)

    def finish_first(k, quarters, halves):
        def action(start, rows_of):
            value = placed(start, halves)
            for c in quarters:
                conv_first[c, rows_of, :] = value[:, cut(c)]

            @pl.when(encoder)
            def _():
                for c in quarters:
                    g[k + 1, me, c, rows_of, :] = silu(value[:, cut(c)])
        over_rows(action)

    def finish_second(t, quarters, halves):
        def action(start, rows_of):
            value = placed(start, halves)

            @pl.when(encoder)
            def _():
                for c in quarters:
                    passed_out[t, c, rows_of, :] = g[2 * t, me, c, rows_of, :] + value[:, cut(c)]

            @pl.when(jnp.logical_not(encoder))
            def _():
                for c in quarters:
                    passed_out[t, c, rows_of, :] = silu(conv_first[c, rows_of, :] + value[:, cut(c)])
        over_rows(action)

    for c in range(QUARTERS):
        g[0, me, c] = resident[:, cut(c)]

        @pl.when(jnp.logical_not(encoder))
        def _():
            g[1, me, c] = held_skip[:, cut(c)]

    send_early(0)
    for t in range(ticks):
        k = 2 * t

        def input_ready(unit):
            if t:
                @pl.when(seg > 0)
                def _():
                    give(t - 1, 0, unit).wait_recv()

        def operand_ready(unit):
            if t:
                @pl.when(jnp.logical_not(encoder))
                def _():
                    give(t - 1, 1, unit).wait_recv()

        def early_first():
            finish_first(k, (0,), 1)
            if t == 0:
                send_early(1)
            else:
                @pl.when(jnp.logical_not(shares_input))
                def _():
                    operand_ready(0)
                    send_early(k + 1)

        def early_second():
            finish_second(t, (0,), 1)
            if t < ticks - 1:
                give_unit(t, 0)

                @pl.when(seg == 0)
                def _():
                    for c in range(QUARTERS):
                        g[k + 2, me, c] = fresh[t, :, cut(c)]
                    send_early(k + 2)

        if t:
            @pl.when(seg > 0)
            def _():
                give(t - 1, 0, 0).wait_recv()
                send_early(k)

        gather_and_multiply(k, 0, input_ready, early_first)
        finish_first(k, (1, 2, 3), 2)

        if t == 0:
            gather_and_multiply(1, 1, operand_ready, early_second)
        else:
            @pl.when(shares_input)
            def _():
                multiply_held(k, 1, early_second)

            @pl.when(jnp.logical_not(shares_input))
            def _():
                gather_and_multiply(k + 1, 1, operand_ready, early_second)
        finish_second(t, (1, 2, 3), 2)
        if t < ticks - 1:
            give_unit(t, 1)
            give_unit(t, 2)

    for t in range(ticks - 1):
        for unit in range(len(UNITS)):
            @pl.when(seg < segments - 1)
            def _():
                give(t, 0, unit).wait_send()

            @pl.when(seg < half - 1)
            def _():
                give(t, 1, unit).wait_send()
    for c in range(QUARTERS):
        out_ref[:, cut(c)] = passed_out[ticks - 1, c]


def body(segments, n, resident, held_skip, fresh, first_weight, second_weight):
    ticks = fresh.shape[0] + 1
    rows, positions = resident.shape[1:]
    quarter = positions // QUARTERS
    length = n // 2
    width = 2 * rows
    vmem = pl.BlockSpec(memory_space=pltpu.VMEM)
    anywhere = pl.BlockSpec(memory_space=pl.ANY)
    out = pl.pallas_call(
        functools.partial(kernel, segments, n, ticks),
        out_shape=jax.ShapeDtypeStruct((rows, positions), jnp.float32),
        in_specs=[vmem, vmem, vmem, anywhere, anywhere],
        out_specs=vmem,
        scratch_shapes=[
            pltpu.VMEM((9, rows, length * width), jnp.float32),
            pltpu.VMEM((2, length, 3, 3 * rows, 3 * width), jnp.bfloat16),
            pltpu.VMEM((2 * ticks, n, QUARTERS, rows, quarter), jnp.float32),
            pltpu.VMEM((3 * width, 2 * quarter), jnp.bfloat16),
            pltpu.VMEM((HALVES, 3, 3 * rows, 2 * quarter), jnp.float32),
            pltpu.VMEM((QUARTERS, rows, quarter), jnp.float32),
            pltpu.VMEM((ticks, QUARTERS, rows, quarter), jnp.float32),
            pltpu.SemaphoreType.DMA((9,)),
            pltpu.SemaphoreType.DMA((2 * ticks, n, len(UNITS))),
            pltpu.SemaphoreType.DMA((2, 3, n, len(UNITS))),
            pltpu.SemaphoreType.DMA((2, length)),
            pltpu.SemaphoreType.DMA((ticks - 1, 2, len(UNITS))),
            pltpu.SemaphoreType.DMA((ticks - 1, 2, len(UNITS))),
        ],
        compiler_params=pltpu.CompilerParams(
            collective_id=0, has_side_effects=True, vmem_limit_bytes=62 * 1024 * 1024
        ),
    )(resident[0], held_skip[0], fresh, first_weight, second_weight)
    return out[None]


def solution(mesh):
    return jax.shard_map(
        functools.partial(body, mesh.shape["segment"], mesh.shape["chan"]),
        mesh=mesh,
        in_specs=(
            P("segment", "chan", None),
            P("segment", "chan", None),
            P(None, "chan", None),
            P("segment", "chan", None),
            P("segment", "chan", None),
        ),
        out_specs=P("segment", "chan", None),
        check_vma=False,
    )
```

time: 174 us -> 176 us (1.011)
  Pallas kernels: 172 us -> 174 us
    pallas_call x1, Pallas kernels: 172 us -> 174 us  [body(): pl.pallas_call(functools.partial(kernel, segments, n, ticks), out_shape=j...]
where the time goes in v3:
time: 176 us
  Pallas kernels  174 us (99%)
    pallas_call x1, Pallas kernels, body(): pl.pallas_call(functools.partial(kernel, segments, n, ticks), out_shape=j...  174 us

profile of v3, /device:TPU:3, one launch (start us, length us, event | category | flops | bytes accessed | tf_op | source)
XLA Modules:
  0.0 175.9 jit_solution(5610971160906968515)
XLA Ops:
  0.0 174.2 %shard_map.55 = f32[160,512]{1,0:T(8,128)} custom-call(f32[160,512]{1,0:T(8,128)} %bitcast.4, f32[160,512]{1,0:T(8,128)} %bitcast.5, f32[2,160,512]{2,1,0:T(8,128)} %fresh.1, f32[1,160,11520]{2,1,0:T(8,128)} %first_weight.1, f32[1,160,11520]{2,1,0:T(8,128)} %second_weight.1), custom_call_target="tpu_custom_call" | custom-call | tf_op jit(solution)/shard_map/pallas_call | solution.py:432
  174.2 1.7 copy.7

commit v4 on v2

--- a/solution.py
+++ b/solution.py
@@ -110,7 +110,7 @@
         return pltpu.make_async_remote_copy(
             src_ref=g.at[k, j, h],
             dst_ref=g.at[k, j, h],
-            send_sem=send_sem.at[way, j, h],
+            send_sem=send_sem.at[k % 2, way, j, h],
             recv_sem=recv_sem.at[k, j, h],
             device_id=(seg, target),
             device_id_type=MESH,
@@ -147,7 +147,26 @@
             return 0
         lax.fori_loop(0, 3, group, 0)
 
+    def drain(k):
+        def one(u, _):
+            q = u // HALVES
+            h = u % HALVES
+            j = 2 * q + core
+            hop(k, j, h, 2).wait_send()
+
+            @pl.when((q <= place) & (place < length - 1))
+            def _():
+                hop(k, j, h, 1).wait_send()
+
+            @pl.when((q >= place) & (place > 0))
+            def _():
+                hop(k, j, h, 0).wait_send()
+            return 0
+        lax.fori_loop(0, length * HALVES, one, 0)
+
     def gather_and_multiply(k, conv, ready):
+        if k >= 2:
+            drain(k - 2)
         for h in range(HALVES):
             ready(h)
 
@@ -201,22 +220,6 @@
             lax.fori_loop(0, 2, one, 0)
             return 0
         lax.fori_loop(HALVES, length * HALVES, step, 0)
-
-        def drain(u, _):
-            q = u // HALVES
-            h = u % HALVES
-            j = 2 * q + core
-            hop(k, j, h, 2).wait_send()
-
-            @pl.when((q <= place) & (place < length - 1))
-            def _():
-                hop(k, j, h, 1).wait_send()
-
-            @pl.when((q >= place) & (place > 0))
-            def _():
-                hop(k, j, h, 0).wait_send()
-            return 0
-        lax.fori_loop(0, length * HALVES, drain, 0)
 
     def multiply_held(k, conv):
         for h in range(HALVES):
@@ -307,6 +310,8 @@
 
             @pl.when(shares_input)
             def _():
+                if t == 1:
+                    drain(1)
                 multiply_held(k, 1)
 
             @pl.when(jnp.logical_not(shares_input))
@@ -337,6 +342,12 @@
             def _():
                 for h in range(HALVES):
                     give(t, 1, h).start()
+
+    drain(2 * ticks - 2)
+
+    @pl.when(jnp.logical_not(shares_input) | (ticks == 1))
+    def _():
+        drain(2 * ticks - 1)
 
     for t in range(ticks - 1):
         for h in range(HALVES):
@@ -374,7 +385,7 @@
             pltpu.VMEM((ticks, HALVES, rows, part_positions), jnp.float32),
             pltpu.SemaphoreType.DMA((9,)),
             pltpu.SemaphoreType.DMA((2 * ticks, n, HALVES)),
-            pltpu.SemaphoreType.DMA((3, n, HALVES)),
+            pltpu.SemaphoreType.DMA((2, 3, n, HALVES)),
             pltpu.SemaphoreType.DMA((ticks - 1, 2, HALVES)),
             pltpu.SemaphoreType.DMA((ticks - 1, 2, HALVES)),
         ],

time: 174 us -> 174 us (level)
  no operation moved by 1% of the time
where the time goes in v4:
time: 174 us
  Pallas kernels  172 us (99%)
    pallas_call x1, Pallas kernels, body(): pl.pallas_call(functools.partial(kernel, segments, n, ticks), out_shape=j...  172 us

profile of v4, /device:TPU:3, one launch (start us, length us, event | category | flops | bytes accessed | tf_op | source)
XLA Modules:
  0.0 174.0 jit_solution(9129352561183103158)
XLA Ops:
  0.0 172.3 %shard_map.55 = f32[160,512]{1,0:T(8,128)} custom-call(f32[160,512]{1,0:T(8,128)} %bitcast.4, f32[160,512]{1,0:T(8,128)} %bitcast.5, f32[2,160,512]{2,1,0:T(8,128)} %fresh.1, f32[1,160,11520]{2,1,0:T(8,128)} %first_weight.1, f32[1,160,11520]{2,1,0:T(8,128)} %second_weight.1), custom_call_target="tpu_custom_call" | custom-call | tf_op jit(solution)/shard_map/pallas_call | solution.py:373
  172.3 1.7 copy.7

commit v5 on v4

--- a/solution.py
+++ b/solution.py
@@ -191,35 +191,32 @@
             return 0
         lax.fori_loop(0, HALVES, own, 0)
 
+        inner = jnp.where(place < length // 2, 1, -1)
+
         def step(u, _):
-            d = u // HALVES
+            d = u // (2 * HALVES) + 1
+            turn = (u // HALVES) % 2
             h = u % HALVES
-            for side in range(2):
-                q = place - d if side == 0 else place + d
-                there = q >= 0 if side == 0 else q < length
-                onward = place < length - 1 if side == 0 else place > 0
-                mine = 2 * q + core
-
-                @pl.when(there)
+            way = jnp.where(turn == 0, inner, -inner)
+            q = place + way * d
+            mine = 2 * q + core
+
+            @pl.when((q >= 0) & (q < length))
+            def _():
+                hop(k, mine, h, 2).wait_recv()
+
+                @pl.when((way > 0) & (place > 0))
                 def _():
-                    hop(k, mine, h, 2).wait_recv()
-
-                    @pl.when(onward)
-                    def _():
-                        hop(k, mine, h, 1 - side).start()
-                    hop(k, mine, h, 2).start()
-
-            def one(side, _):
-                q = place - d + 2 * d * side
-
-                @pl.when((q >= 0) & (q < length))
+                    hop(k, mine, h, 0).start()
+
+                @pl.when((way < 0) & (place < length - 1))
                 def _():
-                    hop(k, 2 * q + 1 - core, h, 2).wait_recv()
-                    multiply(k, conv, q, h, False)
-                return 0
-            lax.fori_loop(0, 2, one, 0)
-            return 0
-        lax.fori_loop(HALVES, length * HALVES, step, 0)
+                    hop(k, mine, h, 1).start()
+                hop(k, mine, h, 2).start()
+                hop(k, 2 * q + 1 - core, h, 2).wait_recv()
+                multiply(k, conv, q, h, False)
+            return 0
+        lax.fori_loop(0, (length - 1) * 2 * HALVES, step, 0)
 
     def multiply_held(k, conv):
         for h in range(HALVES):

time: 174 us -> 171 us (0.983)
  Pallas kernels: 172 us -> 169 us
    pallas_call x1, Pallas kernels: 172 us -> 169 us  [body(): pl.pallas_call(functools.partial(kernel, segments, n, ticks), out_shape=j...]
where the time goes in v5:
time: 171 us
  Pallas kernels  169 us (99%)
  local copies, waits for them, and re-layouts  1.72 us (1%)
    pallas_call x1, Pallas kernels, body(): pl.pallas_call(functools.partial(kernel, segments, n, ticks), out_shape=j...  169 us

profile of v5, /device:TPU:3, one launch (start us, length us, event | category | flops | bytes accessed | tf_op | source)
XLA Modules:
  0.0 170.6 jit_solution(7124331378782407069)
XLA Ops:
  0.0 168.9 %shard_map.55 = f32[160,512]{1,0:T(8,128)} custom-call(f32[160,512]{1,0:T(8,128)} %bitcast.4, f32[160,512]{1,0:T(8,128)} %bitcast.5, f32[2,160,512]{2,1,0:T(8,128)} %fresh.1, f32[1,160,11520]{2,1,0:T(8,128)} %first_weight.1, f32[1,160,11520]{2,1,0:T(8,128)} %second_weight.1), custom_call_target="tpu_custom_call" | custom-call | tf_op jit(solution)/shard_map/pallas_call | solution.py:370
  168.9 1.7 %copy.7 = f32[1,160,512]{2,1,0:T(8,128)} copy(f32[1,160,512]{2,1,0:T(8,128)} %bitcast.3) | data formatting | bytes 655360
